TPU v7x, 32 devices: a whole 2x2x4 slice. The times are simulated.
32 devices in a mesh: parts: 2 (over y), row: 4 (over z), col: 4 (over x, core), sub: 1.
Axes of the slice: x: 2, y: 2, z: 4, core: 2. Of those that a mesh axis runs over, the one named last changes fastest.
Arguments:
- activations: bfloat16 [1024, 2048], P(('parts', 'row'), ('col', 'sub')), parts along dimension 0, may hold values from -6 to 6
- expert_ids: int32 [1024, 8], P(('parts', 'row')), parts along dimension 0, may hold values from 0 to 15, all different within a row; in each aligned block of 32 rows (0 to 31, 32 to 63, ...) at most 32 rows name the same one
- gate_scores: float32 [1024, 8], P(('parts', 'row')), parts along dimension 0, may hold values from 0.05 to 0.5
- gate_proj: bfloat16 [16, 2048, 768], P(('row', 'col'), None, 'sub'), may hold values from -0.125 to 0.125
- up_proj: bfloat16 [16, 2048, 768], P(('row', 'col'), None, 'sub'), may hold values from -0.125 to 0.125
- down_proj: bfloat16 [16, 768, 2048], P(('row', 'col'), 'sub'), may hold values from -0.21875 to 0.21875
Outputs:
- moe_output: bfloat16 [1024, 2048], P(('parts', 'row'), ('col', 'sub')), parts along dimension 0
There are 2 independent parts, one for each index of `parts`. A program takes and returns all parts, laid end to end along the dimension named above; an argument that names none is the same for every part. Nothing has to cross between parts.
Inputs may be any that keep to these rules, and one draw needn't show every extreme that they name: `expert_ids`: each row names 8 different experts. In each aligned block of 32 rows no expert is named by more than 32 rows, a bound that some block reaches.
All inputs are finite; a program needn't handle non-finite values.
Results may differ from a plain program's by a relative error of at most 0.0057.
Values may be sent and summed in bfloat16 or wider, within the bound.
No kernel may reach another device: no remote copies, remote signals or barrier semaphores. Data moves between devices by JAX's collectives and lax.ppermute only.
A program may use at most 64 MiB of HBM per device.

v0:
```python
import jax
import jax.numpy as jnp
from jax import lax
from jax.sharding import PartitionSpec as P

TOP = 8


def slot_places(chosen, experts, capacity):
    count = chosen.shape[0] * chosen.shape[1]
    flat_ids = chosen.reshape(count)
    onehot = (flat_ids[:, None] == jnp.arange(experts, dtype=jnp.int32)[None, :]).astype(jnp.int32)
    running = jnp.cumsum(onehot, axis=0) - 1
    ranking = jnp.sum(onehot * running, axis=1)
    return flat_ids * capacity + ranking


def fill_slots(row_block, places, experts, capacity, top_count):
    owners = jnp.full((experts * capacity,), row_block.shape[0], jnp.int32)
    owners = owners.at[places].set(jnp.arange(places.shape[0], dtype=jnp.int32) // top_count)
    padded = jnp.concatenate(
        [row_block, jnp.zeros((1, row_block.shape[1]), row_block.dtype)], axis=0
    )
    return padded[owners].reshape(experts, capacity, row_block.shape[1])


def run_expert(stacked, gate_proj, up_proj, down_proj):
    layout = stacked.shape
    inputs = stacked.reshape(-1, layout[-1])
    gate_val = jnp.dot(inputs, gate_proj[0], preferred_element_type=jnp.float32)
    up_val = jnp.dot(inputs, up_proj[0], preferred_element_type=jnp.float32)
    hidden = (jax.nn.silu(gate_val) * up_val).astype(jnp.bfloat16)
    partial_out = jnp.dot(hidden, down_proj[0], preferred_element_type=jnp.float32)
    return partial_out.reshape(layout)


def send_back(stacked, gate_proj, up_proj, down_proj):
    partial_out = run_expert(stacked, gate_proj, up_proj, down_proj)
    landed = lax.all_to_all(partial_out, ("row", "col"), split_axis=1, concat_axis=1, tiled=True)
    return lax.psum_scatter(landed, "sub", scatter_dimension=0, tiled=True).astype(jnp.bfloat16)


def per_device(activations, expert_ids, gate_scores, gate_proj, up_proj, down_proj):
    col_count = lax.axis_size("col")
    sub_count = lax.axis_size("sub")
    experts = lax.axis_size("row") * col_count
    group_rows = expert_ids.shape[0]
    block_rows = group_rows // (col_count * sub_count)
    capacity = max(2, min(block_rows, 2 * block_rows * TOP // experts))
    quarter = sub_count * block_rows
    width = activations.shape[1] * col_count * sub_count
    whole = lax.all_gather(activations, ("col", "sub"), axis=1, tiled=True)
    col_start = lax.axis_index("col") * quarter
    sub_index = lax.axis_index("sub")
    my_rows = lax.dynamic_slice_in_dim(whole, col_start, quarter, 0)
    my_ids = lax.dynamic_slice_in_dim(expert_ids, col_start, quarter, 0)
    own_scores = lax.dynamic_slice_in_dim(
        gate_scores, col_start + sub_index * block_rows, block_rows, 0
    )
    places = []
    for member in range(sub_count):
        lower = member * block_rows
        places.append(slot_places(my_ids[lower : lower + block_rows], experts, capacity))
    own_places = lax.dynamic_index_in_dim(jnp.stack(places), sub_index, 0, keepdims=False)
    buffers = []
    for member in range(sub_count):
        lower = member * block_rows
        buffers.append(
            fill_slots(my_rows[lower : lower + block_rows], places[member], experts, capacity, TOP)
        )
    outgoing = jnp.stack(buffers)
    returned = send_back(
        lax.all_to_all(outgoing, ("row", "col"), split_axis=1, concat_axis=1, tiled=True),
        gate_proj,
        up_proj,
        down_proj,
    )
    picked = returned.reshape(-1, width)[own_places].reshape(block_rows, TOP, width)
    share = jnp.sum(own_scores[:, :, None] * picked.astype(jnp.float32), axis=1)
    return lax.all_to_all(
        share.astype(jnp.bfloat16), ("col", "sub"), split_axis=1, concat_axis=0, tiled=True
    )


def solution(mesh):
    placed = (
        P(("parts", "row"), ("col", "sub")),
        P(("parts", "row"), None),
        P(("parts", "row"), None),
        P(("row", "col"), None, "sub"),
        P(("row", "col"), None, "sub"),
        P(("row", "col"), "sub", None),
    )
    return jax.shard_map(
        per_device,
        mesh=mesh,
        in_specs=placed,
        out_specs=P(("parts", "row"), ("col", "sub")),
        check_vma=False,
    )
```

profile of v0, /device:TPU:20, one launch (start us, length us, event | category | flops | bytes accessed | tf_op | source)
XLA Modules:
  0.0 142.7 jit_solution(10261888234593727119)
XLA Ops:
  0.0 0.9 broadcast_multiply_fusion
  0.9 0.1 copy.21
  1.0 0.1 eq.29
  1.1 0.1 eq.25
  1.2 0.6 reduce-window.6
  1.8 0.2 slice_reduce_fusion
  2.0 0.1 copy.20
  2.1 0.1 mul.43
  2.2 0.1 fusion.9
  2.3 1.4 scatter_custom_fusion
  3.7 7.4 %all_gather.3 = bf16[128,2048]{1,0:T(8,128)(2,1)S(1)} all-gather(bf16[128,512]{1,0:T(8,128)(2,1)} %param.6), channel_id=1, replica_groups=mesh['parts'=2,'row'=4,'col'=4,'sub'=1] {'col','sub'}, dimensions={1}, use_global_device_ids=true | all-gather | bytes 655360 | tf_op jit(solution)/shard_map/all_gather | solution.py:52
  11.1 3.3 %gather_fusion = bf16[512,2048]{1,0:T(8,128)(2,1)} fusion(bf16[33,2048]{1,0:T(8,128)(2,1)S(1)} %concatenate.3, s32[1024]{0:T(1024)S(1)} %pad_clamp_fusion.1), kind=kCustom, calls=%fused_computation | custom fusion | bytes 4196352 | tf_op jit(solution)/shard_map/gather | solution.py:24
  14.5 53.6 %all_to_all.26 = bf16[1,16,32,2048]{3,2,0,1:T(8,128)(2,1)S(1)} all-to-all(bf16[1,16,32,2048]{3,2,0,1:T(8,128)(2,1)} %bitcast.52), channel_id=1, replica_groups=mesh['parts'=2,'row'=4,'col'=4,'sub'=1] {'row','col'}, dimensions={1} | all-to-all | bytes 4194304 | tf_op jit(solution)/shard_map/all_to_all | solution.py:73
  68.1 1.8 %fusion.3 = f32[512,768]{1,0:T(8,128)S(1)} fusion(bf16[512,2048]{1,0:T(8,128)(2,1)S(1)} %bitcast.53, bf16[1,2048,768]{2,1,0:T(8,128)(2,1)S(1)} %copy-done.2), kind=kOutput, calls=%fused_computation.7 | convolution fusion | flops 1610612736 | bytes 6815744 | tf_op jit(solution)/shard_map/dot_general | solution.py:30
  69.9 1.9 %multiply_convert_fusion = bf16[512,768]{1,0:T(8,128)(2,1)S(1)} fusion(f32[512,768]{1,0:T(8,128)S(1)} %fusion.3, bf16[512,2048]{1,0:T(8,128)(2,1)S(1)} %bitcast.54, bf16[1,2048,768]{2,1,0:T(8,128)(2,1)S(1)} %copy-done.3), kind=kOutput, calls=%fused_computation.11 | convolution fusion | flops 1612972032 | bytes 7602176 | tf_op jit(solution)/shard_map/dot_general | solution.py:31
  71.9 3.1 %convolution_bitcast_fusion = bf16[1,16,32,2048]{3,2,0,1:T(8,128)(2,1)} fusion(bf16[16,32,768]{2,1,0:T(8,128)(2,1)S(1)} %bitcast.61, bf16[1,768,2048]{2,1,0:T(8,128)(2,1)S(1)} %copy-done), kind=kOutput, calls=%fused_computation.3 | convolution fusion | flops 1610612736 | bytes 6029312 | tf_op jit(solution)/shard_map/dot_general | solution.py:33
  75.0 4.9 %all-to-all-start.1 = ((bf16[1,16,32,2048]{3,2,0,1:T(8,128)(2,1)}), bf16[1,16,32,2048]{3,2,0,1:T(8,128)(2,1)}, u32[]{:S(2)}, u32[]{:S(2)}) async-start(bf16[1,16,32,2048]{3,2,0,1:T(8,128)(2,1)} %convolution_bitcast_fusion), calls=%async_computation.1 | async-start | bytes 4194304 | tf_op jit(solution)/shard_map/all_to_all | solution.py:39
  79.9 0.1 constant_dynamic-slice_fusion.2
  80.0 0.1 copy.19
  80.0 47.6 %all-to-all-done.1 = bf16[1,16,32,2048]{3,2,0,1:T(8,128)(2,1)} async-done(((bf16[1,16,32,2048]{3,2,0,1:T(8,128)(2,1)}), bf16[1,16,32,2048]{3,2,0,1:T(8,128)(2,1)}, u32[]{:S(2)}, u32[]{:S(2)}) %all-to-all-start.1) | async-done | bytes 2097184 | tf_op jit(solution)/shard_map/all_to_all | solution.py:39
  127.6 5.2 %gather_fusion.1 = bf16[256,2048]{1,0:T(8,128)(2,1)} fusion(bf16[512,2048]{1,0:T(8,128)(2,1)} %bitcast.13, s32[1024]{0:T(1024)S(1)} %pad_clamp_fusion), kind=kCustom, calls=%fused_computation.1 | custom fusion | bytes 2098176 | tf_op jit(solution)/shard_map/gather | solution.py:78
  132.8 2.2 %fusion.5 = bf16[32,2048]{1,0:T(8,128)(2,1)S(1)} fusion(bf16[256,2048]{1,0:T(8,128)(2,1)} %gather_fusion.1, f32[32,8]{1,0:T(8,128)S(1)} %copy.19), kind=kLoop, calls=%fused_computation.10 | loop fusion | flops 1507328 | bytes 1180672 | tf_op jit(solution)/shard_map/reduce_sum | solution.py:79
  135.0 7.0 %all_to_all.27 = bf16[32,4,512]{2,0,1:T(8,128)(2,1)S(1)} all-to-all(bf16[32,4,512]{2,0,1:T(8,128)(2,1)S(1)} %bitcast.56), channel_id=1, replica_groups=mesh['parts'=2,'row'=4,'col'=4,'sub'=1] {'col','sub'}, dimensions={1} | all-to-all | bytes 262144 | tf_op jit(solution)/shard_map/all_to_all | solution.py:80
  142.0 0.7 copy.33
  (19 shorter events, 0.2 us)
Async XLA Ops:
  0.0 71.9 %copy-start = (bf16[1,768,2048]{2,1,0:T(8,128)(2,1)S(1)}, bf16[1,768,2048]{2,1,0:T(8,128)(2,1)}, u32[]{:S(2)}) copy-start(bf16[1,768,2048]{2,1,0:T(8,128)(2,1)} %param.11) | copy-start | bytes 9437188
  14.5 53.6 %copy-start.2 = (bf16[1,2048,768]{2,1,0:T(8,128)(2,1)S(1)}, bf16[1,2048,768]{2,1,0:T(8,128)(2,1)}, u32[]{:S(2)}) copy-start(bf16[1,2048,768]{2,1,0:T(8,128)(2,1)} %param.9) | copy-start | bytes 9437188
  68.1 1.9 %copy-start.3 = (bf16[1,2048,768]{2,1,0:T(8,128)(2,1)S(1)}, bf16[1,2048,768]{2,1,0:T(8,128)(2,1)}, u32[]{:S(2)}) copy-start(bf16[1,2048,768]{2,1,0:T(8,128)(2,1)} %param.10) | copy-start | bytes 9437188
  75.0 4.9 %copy-start.1 = (f32[128,8]{0,1:T(8,128)S(1)}, f32[128,8]{0,1:T(8,128)}, u32[]{:S(2)}) copy-start(f32[128,8]{0,1:T(8,128)} %param.8) | copy-start | bytes 12292
  75.0 52.6 %all-to-all-start.1 = ((bf16[1,16,32,2048]{3,2,0,1:T(8,128)(2,1)}), bf16[1,16,32,2048]{3,2,0,1:T(8,128)(2,1)}, u32[]{:S(2)}, u32[]{:S(2)}) async-start(bf16[1,16,32,2048]{3,2,0,1:T(8,128)(2,1)} %convolution_bitcast_fusion), calls=%async_computation.1 | async-start | bytes 4194304 | tf_op jit(solution)/shard_map/all_to_all | solution.py:39
where the time goes:
time: 143 us
  blocking collectives  67.9 us (47%)
  waiting for transfers between devices  47.6 us (33%)
  local copies, waits for them, and re-layouts  11.5 us (8%)
  matrix products  6.85 us (5%)
  starting transfers between devices  4.86 us (3%)
  other arithmetic  3.86 us (3%)
    all_to_all x1, blocking collectives, per_device(): lax.all_to_all(outgoing, ('row', 'col'), split_axis=1, concat_axis=1, til...  53.6 us
    all_to_all x1, waiting for transfers between devices, send_back(): lax.all_to_all(partial_out, ('row', 'col'), split_axis=1, concat_axis=1,...  47.6 us
    all_gather x1, blocking collectives, per_device(): whole = lax.all_gather(activations, ('col', 'sub'), axis=1, tiled=True)  7.38 us
    all_to_all x1, blocking collectives, per_device(): lax.all_to_all(share.astype(jnp.bfloat16), ('col', 'sub'), split_axis=1,...  6.99 us
    gather x1, local copies, waits for them, and re-layouts, per_device(): returned.reshape(-1, width)[own_places].reshape(block_rows, TOP, width)  5.21 us
    all_to_all x1, starting transfers between devices, send_back(): lax.all_to_all(partial_out, ('row', 'col'), split_axis=1, concat_axis=1,...  4.86 us
    gather x1, local copies, waits for them, and re-layouts, fill_slots(): return padded[owners].reshape(experts, capacity, row_block.shape[1])  3.35 us
    dot_general x1, matrix products, run_expert(): jnp.dot(hidden, down_proj[0], preferred_element_type=jnp.float32)  3.14 us
  transfers between devices with their start and end apart: 1, of which 1 were waited for; matrix products, arithmetic and copies ran while one was open for 0% of the time, Pallas kernels for 0%

commit v1 on v0

--- a/solution.py
+++ b/solution.py
@@ -4,6 +4,36 @@
 from jax.sharding import PartitionSpec as P
 
 TOP = 8
+
+
+def _recast_heads(original, dim_k, panel):
+    view_out = original.shape
+    e_now = original.reshape(
+        *view_out[:dim_k], panel, view_out[dim_k] // panel, *view_out[dim_k + 1 :]
+    )
+    upper = jnp.moveaxis(e_now, dim_k, 0)
+    return upper
+
+
+def begin_inputs(mine, at_axis):
+    mine = jnp.moveaxis(mine, 0, at_axis)
+    piece_out = mine.shape
+    y2 = mine.reshape(
+        *piece_out[:at_axis], piece_out[at_axis] * piece_out[at_axis + 1], *piece_out[at_axis + 2 :]
+    )
+    return y2
+
+
+def see_the_blocks(z, group_axis, t0, values):
+    then, response = (lax.axis_size(group_axis), lax.axis_index(group_axis))
+    small = _recast_heads(z, t0, then)
+    xs_all = [small[response]]
+    for j in range(1, then):
+        all_rows = small[response ^ j]
+        xs_all.append(lax.ppermute(all_rows, group_axis, perm=[(pp, pp ^ j) for pp in range(then)]))
+    small = jnp.stack(xs_all)[response ^ jnp.arange(then)]
+    wide_out = begin_inputs(small, values)
+    return wide_out
 
 
 def slot_places(chosen, experts, capacity):
@@ -70,10 +100,7 @@
         )
     outgoing = jnp.stack(buffers)
     returned = send_back(
-        lax.all_to_all(outgoing, ("row", "col"), split_axis=1, concat_axis=1, tiled=True),
-        gate_proj,
-        up_proj,
-        down_proj,
+        see_the_blocks(outgoing, ("row", "col"), 1, 1), gate_proj, up_proj, down_proj
     )
     picked = returned.reshape(-1, width)[own_places].reshape(block_rows, TOP, width)
     share = jnp.sum(own_scores[:, :, None] * picked.astype(jnp.float32), axis=1)

time: 143 us -> 157 us (1.098)
  blocking collectives: 67.9 us -> 14.4 us
  waiting for transfers between devices: 47.6 us -> 75.2 us
  starting transfers between devices: 4.86 us -> 25.7 us
  local copies, waits for them, and re-layouts: 11.5 us -> 27.3 us
  matrix products: 6.85 us -> 9.5 us
    all_to_all x1 -> x0, blocking collectives: 53.6 us -> none  [per_device(): lax.all_to_all(outgoing, ('row', 'col'), split_axis=1, concat_axis=1, til...]
    ppermute x0 -> x15, waiting for transfers between devices: none -> 27.7 us  [see_the_blocks(): lax.ppermute(all_rows, group_axis, perm=[(pp, pp ^ j) for pp in range(the...]
    ppermute x0 -> x15, starting transfers between devices: none -> 21 us  [see_the_blocks(): lax.ppermute(all_rows, group_axis, perm=[(pp, pp ^ j) for pp in range(the...]
    unnamed x9 -> x23, local copies, waits for them, and re-layouts: 0.74 us -> 9.92 us
    gather x0 -> x1, local copies, waits for them, and re-layouts: none -> 3.58 us  [see_the_blocks(): small = jnp.stack(xs_all)[response ^ jnp.arange(then)]]
    dot_general x1, matrix products: 1.81 us -> 4.45 us  [run_expert(): gate_val = jnp.dot(inputs, gate_proj[0], preferred_element_type=jnp.float32)]
    squeeze x0 -> x1, local copies, waits for them, and re-layouts: none -> 2.42 us  [see_the_blocks(): all_rows = small[response ^ j]]
  transfers between devices with their start and end apart: 1 -> 16, of which waited for: 1 -> 9; matrix products, arithmetic and copies ran while one was open for 0% -> 6% of each run, Pallas kernels for 0% -> 0%
where the time goes in v1:
time: 157 us; the launch traced here: 156 us
  waiting for transfers between devices  75.2 us (48%)
  local copies, waits for them, and re-layouts  27.3 us (17%)
  starting transfers between devices  25.7 us (16%)
  blocking collectives  14.4 us (9%)
  matrix products  9.5 us (6%)
  other arithmetic  3.87 us (2%)
    all_to_all x1, waiting for transfers between devices, send_back(): lax.all_to_all(partial_out, ('row', 'col'), split_axis=1, concat_axis=1,...  47.6 us
    ppermute x15, waiting for transfers between devices, see_the_blocks(): lax.ppermute(all_rows, group_axis, perm=[(pp, pp ^ j) for pp in range(the...  27.7 us
    ppermute x15, starting transfers between devices, see_the_blocks(): lax.ppermute(all_rows, group_axis, perm=[(pp, pp ^ j) for pp in range(the...  21 us
    unnamed x23, local copies, waits for them, and re-layouts  9.92 us
    all_gather x1, blocking collectives, per_device(): whole = lax.all_gather(activations, ('col', 'sub'), axis=1, tiled=True)  7.38 us
    all_to_all x1, blocking collectives, per_device(): lax.all_to_all(share.astype(jnp.bfloat16), ('col', 'sub'), split_axis=1,...  6.99 us
    gather x1, local copies, waits for them, and re-layouts, per_device(): returned.reshape(-1, width)[own_places].reshape(block_rows, TOP, width)  5.23 us
    all_to_all x1, starting transfers between devices, send_back(): lax.all_to_all(partial_out, ('row', 'col'), split_axis=1, concat_axis=1,...  4.72 us
  transfers between devices with their start and end apart: 16, of which 9 were waited for; matrix products, arithmetic and copies ran while one was open for 6% of the time, Pallas kernels for 0%

profile of v1, /device:TPU:20, one launch (start us, length us, event | category | flops | bytes accessed | tf_op | source)
XLA Modules:
  0.0 156.2 jit_solution(4643887677983675680)
XLA Ops:
  3.8 7.4 %all_gather.3 = bf16[128,2048]{1,0:T(8,128)(2,1)S(1)} all-gather(bf16[128,512]{1,0:T(8,128)(2,1)} %param.6), channel_id=1, replica_groups=mesh['parts'=2,'row'=4,'col'=4,'sub'=1] {'col','sub'}, dimensions={1}, use_global_device_ids=true | all-gather | bytes 655360 | tf_op jit(solution)/shard_map/all_gather | solution.py:82
  11.2 3.3 %gather_fusion = bf16[512,2048]{1,0:T(8,128)(2,1)} fusion(bf16[33,2048]{1,0:T(8,128)(2,1)S(1)} %concatenate.3, s32[1024]{0:T(1024)S(1)} %pad_clamp_fusion.2), kind=kCustom, calls=%fused_computation | custom fusion | bytes 4196352 | tf_op jit(solution)/shard_map/gather | solution.py:54
  14.5 2.4 %dynamic-slice_bitcast_fusion = (bf16[1,1,32,2048]{3,2,1,0:T(8,128)(2,1)S(1)}, bf16[1,1,32,2048]{3,2,1,0:T(8,128)(2,1)S(1)}, bf16[1,1,32,2048]{3,2,1,0:T(8,128)(...) fusion(bf16[16,1,1,32,2048]{4,3,0,2,1:T(8,128)(2,1)} %bitcast.1, ...), kind=kLoop, calls=%fused_computation.29 | loop fusion | bytes 4194368 | tf_op jit(solution)/shard_map/squeeze | solution.py:32
  20.8 2.2 %collective-permute-start.5 = (bf16[1,1,32,2048]{3,2,1,0:T(8,128)(2,1)S(1)}, bf16[1,1,32,2048]{3,2,1,0:T(8,128)(2,1)S(1)}, u32[]{:S(2)}, u32[]{:S(2)}) collective-permute-start(bf16[1,1,32,2048]{3,2,1,0:T(8,128)(2,1)S(1)} %get-tuple-element.16), channel_id=1, source_target_pairs={{0,6},{1,7},{2,4},{3,5},{4,2},{5,3},{6,0},{7,1},{8,14},{9,15},{10,... | collective-permute-start | bytes 393224 | tf_op jit(solution)/shard_map/ppermute | solution.py:33
  25.8 3.6 %collective-permute-start.8 = (bf16[1,1,32,2048]{3,2,1,0:T(8,128)(2,1)S(1)}, bf16[1,1,32,2048]{3,2,1,0:T(8,128)(2,1)S(1)}, u32[]{:S(2)}, u32[]{:S(2)}) collective-permute-start(bf16[1,1,32,2048]{3,2,1,0:T(8,128)(2,1)S(1)} %get-tuple-element.13), channel_id=1, source_target_pairs={{0,9},{1,8},{2,11},{3,10},{4,13},{5,12},{6,15},{7,14},{8,1},{9,0},... | collective-permute-start | bytes 393224 | tf_op jit(solution)/shard_map/ppermute | solution.py:33
  31.5 2.2 %collective-permute-done.5 = bf16[1,1,32,2048]{3,2,1,0:T(8,128)(2,1)S(1)} collective-permute-done((bf16[1,1,32,2048]{3,2,1,0:T(8,128)(2,1)S(1)}, bf16[1,1,32,2048]{3,2,1,0:T(8,128)(2,1)S(1)}, u32[]{:S(2)}, u32[]{:S(2)}) %collective-permute-start.5) | collective-permute-done | bytes 131104 | tf_op jit(solution)/shard_map/ppermute | solution.py:33
  33.7 3.4 %collective-permute-start.10 = (bf16[1,1,32,2048]{3,2,1,0:T(8,128)(2,1)S(1)}, bf16[1,1,32,2048]{3,2,1,0:T(8,128)(2,1)S(1)}, u32[]{:S(2)}, u32[]{:S(2)}) collective-permute-start(bf16[1,1,32,2048]{3,2,1,0:T(8,128)(2,1)S(1)} %get-tuple-element.11), channel_id=1, source_target_pairs={{0,11},{1,10},{2,9},{3,8},{4,15},{5,14},{6,13},{7,12},{8,3},{9,2},... | collective-permute-start | bytes 393224 | tf_op jit(solution)/shard_map/ppermute | solution.py:33
  38.9 1.9 %collective-permute-start.12 = (bf16[1,1,32,2048]{3,2,1,0:T(8,128)(2,1)S(1)}, bf16[1,1,32,2048]{3,2,1,0:T(8,128)(2,1)S(1)}, u32[]{:S(2)}, u32[]{:S(2)}) collective-permute-start(bf16[1,1,32,2048]{3,2,1,0:T(8,128)(2,1)S(1)} %get-tuple-element.9), channel_id=1, source_target_pairs={{0,13},{1,12},{2,15},{3,14},{4,9},{5,8},{6,11},{7,10},{8,5},{9,4},... | collective-permute-start | bytes 393224 | tf_op jit(solution)/shard_map/ppermute | solution.py:33
  41.5 8.1 %collective-permute-done.8 = bf16[1,1,32,2048]{3,2,1,0:T(8,128)(2,1)S(1)} collective-permute-done((bf16[1,1,32,2048]{3,2,1,0:T(8,128)(2,1)S(1)}, bf16[1,1,32,2048]{3,2,1,0:T(8,128)(2,1)S(1)}, u32[]{:S(2)}, u32[]{:S(2)}) %collective-permute-start.8) | collective-permute-done | bytes 131104 | tf_op jit(solution)/shard_map/ppermute | solution.py:33
  49.6 2.4 %collective-permute-start.13 = (bf16[1,1,32,2048]{3,2,1,0:T(8,128)(2,1)S(1)}, bf16[1,1,32,2048]{3,2,1,0:T(8,128)(2,1)S(1)}, u32[]{:S(2)}, u32[]{:S(2)}) collective-permute-start(bf16[1,1,32,2048]{3,2,1,0:T(8,128)(2,1)S(1)} %get-tuple-element.8), channel_id=1, source_target_pairs={{0,14},{1,15},{2,12},{3,13},{4,10},{5,11},{6,8},{7,9},{8,6},{9,7},... | collective-permute-start | bytes 393224 | tf_op jit(solution)/shard_map/ppermute | solution.py:33
  55.1 3.0 %collective-permute-done.10 = bf16[1,1,32,2048]{3,2,1,0:T(8,128)(2,1)S(1)} collective-permute-done((bf16[1,1,32,2048]{3,2,1,0:T(8,128)(2,1)S(1)}, bf16[1,1,32,2048]{3,2,1,0:T(8,128)(2,1)S(1)}, u32[]{:S(2)}, u32[]{:S(2)}) %collective-permute-start.10) | collective-permute-done | bytes 131104 | tf_op jit(solution)/shard_map/ppermute | solution.py:33
  58.8 7.2 %collective-permute-done.11 = bf16[1,1,32,2048]{3,2,1,0:T(8,128)(2,1)S(1)} collective-permute-done((bf16[1,1,32,2048]{3,2,1,0:T(8,128)(2,1)S(1)}, bf16[1,1,32,2048]{3,2,1,0:T(8,128)(2,1)S(1)}, u32[]{:S(2)}, u32[]{:S(2)}) %collective-permute-start.11) | collective-permute-done | bytes 131104 | tf_op jit(solution)/shard_map/ppermute | solution.py:33
  66.6 2.1 %collective-permute-done.12 = bf16[1,1,32,2048]{3,2,1,0:T(8,128)(2,1)S(1)} collective-permute-done((bf16[1,1,32,2048]{3,2,1,0:T(8,128)(2,1)S(1)}, bf16[1,1,32,2048]{3,2,1,0:T(8,128)(2,1)S(1)}, u32[]{:S(2)}, u32[]{:S(2)}) %collective-permute-start.12) | collective-permute-done | bytes 131104 | tf_op jit(solution)/shard_map/ppermute | solution.py:33
  69.3 2.8 %collective-permute-done.13 = bf16[1,1,32,2048]{3,2,1,0:T(8,128)(2,1)S(1)} collective-permute-done((bf16[1,1,32,2048]{3,2,1,0:T(8,128)(2,1)S(1)}, bf16[1,1,32,2048]{3,2,1,0:T(8,128)(2,1)S(1)}, u32[]{:S(2)}, u32[]{:S(2)}) %collective-permute-start.13) | collective-permute-done | bytes 131104 | tf_op jit(solution)/shard_map/ppermute | solution.py:33
  72.8 2.0 %collective-permute-done.14 = bf16[1,1,32,2048]{3,2,1,0:T(8,128)(2,1)S(1)} collective-permute-done((bf16[1,1,32,2048]{3,2,1,0:T(8,128)(2,1)S(1)}, bf16[1,1,32,2048]{3,2,1,0:T(8,128)(2,1)S(1)}, u32[]{:S(2)}, u32[]{:S(2)}) %collective-permute-start.14) | collective-permute-done | bytes 131104 | tf_op jit(solution)/shard_map/ppermute | solution.py:33
  75.5 3.6 %gather_fusion.1 = bf16[16,32,2048]{2,1,0:T(8,128)(2,1)} fusion(bf16[16,32,2048]{2,1,0:T(8,128)(2,1)} %bitcast.34, s32[1024]{0:T(1024)S(1)} %pad_clamp_fusion.1), kind=kCustom, calls=%fused_computation.1 | custom fusion | bytes 4194368 | tf_op jit(solution)/shard_map/gather | solution.py:34
  79.1 4.5 %fusion.3 = f32[512,768]{1,0:T(8,128)S(1)} fusion(bf16[512,2048]{1,0:T(8,128)(2,1)} %bitcast.114, bf16[1,2048,768]{2,1,0:T(8,128)(2,1)} %param.9), kind=kOutput, calls=%fused_computation.8 | convolution fusion | flops 1610612736 | bytes 6815744 | tf_op jit(solution)/shard_map/dot_general | solution.py:60
  83.6 1.9 %multiply_convert_fusion = bf16[512,768]{1,0:T(8,128)(2,1)S(1)} fusion(f32[512,768]{1,0:T(8,128)S(1)} %fusion.3, bf16[512,2048]{1,0:T(8,128)(2,1)S(1)} %bitcast.115, bf16[1,2048,768]{2,1,0:T(8,128)(2,1)S(1)} %copy-done.3), kind=kOutput, calls=%fused_computation.12 | convolution fusion | flops 1612972032 | bytes 7602176 | tf_op jit(solution)/shard_map/dot_general | solution.py:61
  85.5 3.2 %convolution_bitcast_fusion = bf16[1,16,32,2048]{3,2,0,1:T(8,128)(2,1)} fusion(bf16[16,32,768]{2,1,0:T(8,128)(2,1)S(1)} %bitcast.122, bf16[1,768,2048]{2,1,0:T(8,128)(2,1)S(1)} %copy-done), kind=kOutput, calls=%fused_computation.4 | convolution fusion | flops 1610612736 | bytes 6029312 | tf_op jit(solution)/shard_map/dot_general | solution.py:63
  88.6 4.7 %all-to-all-start = ((bf16[1,16,32,2048]{3,2,0,1:T(8,128)(2,1)}), bf16[1,16,32,2048]{3,2,0,1:T(8,128)(2,1)}, u32[]{:S(2)}, u32[]{:S(2)}) async-start(bf16[1,16,32,2048]{3,2,0,1:T(8,128)(2,1)} %convolution_bitcast_fusion), calls=%async_computation | async-start | bytes 4194304 | tf_op jit(solution)/shard_map/all_to_all | solution.py:69
  93.5 47.6 %all-to-all-done = bf16[1,16,32,2048]{3,2,0,1:T(8,128)(2,1)} async-done(((bf16[1,16,32,2048]{3,2,0,1:T(8,128)(2,1)}), bf16[1,16,32,2048]{3,2,0,1:T(8,128)(2,1)}, u32[]{:S(2)}, u32[]{:S(2)}) %all-to-all-start) | async-done | bytes 2097184 | tf_op jit(solution)/shard_map/all_to_all | solution.py:69
  141.1 5.2 %gather_fusion.2 = bf16[256,2048]{1,0:T(8,128)(2,1)} fusion(bf16[512,2048]{1,0:T(8,128)(2,1)} %bitcast.44, s32[1024]{0:T(1024)S(1)} %pad_clamp_fusion), kind=kCustom, calls=%fused_computation.2 | custom fusion | bytes 2098176 | tf_op jit(solution)/shard_map/gather | solution.py:105
  146.3 2.2 %fusion.5 = bf16[32,2048]{1,0:T(8,128)(2,1)S(1)} fusion(bf16[256,2048]{1,0:T(8,128)(2,1)} %gather_fusion.2, f32[32,8]{1,0:T(8,128)S(1)} %copy.19), kind=kLoop, calls=%fused_computation.11 | loop fusion | flops 1507328 | bytes 1180672 | tf_op jit(solution)/shard_map/reduce_sum | solution.py:106
  148.5 7.0 %all_to_all.21 = bf16[32,4,512]{2,0,1:T(8,128)(2,1)S(1)} all-to-all(bf16[32,4,512]{2,0,1:T(8,128)(2,1)S(1)} %bitcast.117), channel_id=1, replica_groups=mesh['parts'=2,'row'=4,'col'=4,'sub'=1] {'col','sub'}, dimensions={1} | all-to-all | bytes 262144 | tf_op jit(solution)/shard_map/all_to_all | solution.py:107
  (67 shorter events, 22.2 us)
Async XLA Ops:
  0.0 85.5 %copy-start = (bf16[1,768,2048]{2,1,0:T(8,128)(2,1)S(1)}, bf16[1,768,2048]{2,1,0:T(8,128)(2,1)}, u32[]{:S(2)}) copy-start(bf16[1,768,2048]{2,1,0:T(8,128)(2,1)} %param.11) | copy-start | bytes 9437188
  16.9 3.9 %collective-permute-start = (bf16[1,1,32,2048]{3,2,1,0:T(8,128)(2,1)S(1)}, bf16[1,1,32,2048]{3,2,1,0:T(8,128)(2,1)S(1)}, u32[]{:S(2)}, u32[]{:S(2)}) collective-permute-start(bf16[1,1,32,2048]{3,2,1,0:T(8,128)(2,1)S(1)} %get-tuple-element.21), channel_id=1, source_target_pairs={{0,1},{1,0},{2,3},{3,2},{4,5},{5,4},{6,7},{7,6},{8,9},{9,8},{10,11... | collective-permute-start | bytes 393224 | tf_op jit(solution)/shard_map/ppermute | solution.py:33
  17.3 6.4 %collective-permute-start.1 = (bf16[1,1,32,2048]{3,2,1,0:T(8,128)(2,1)S(1)}, bf16[1,1,32,2048]{3,2,1,0:T(8,128)(2,1)S(1)}, u32[]{:S(2)}, u32[]{:S(2)}) collective-permute-start(bf16[1,1,32,2048]{3,2,1,0:T(8,128)(2,1)S(1)} %get-tuple-element.20), channel_id=1, source_target_pairs={{0,2},{1,3},{2,0},{3,1},{4,6},{5,7},{6,4},{7,5},{8,10},{9,11},{10,... | collective-permute-start | bytes 393224 | tf_op jit(solution)/shard_map/ppermute | solution.py:33
  18.4 6.5 %collective-permute-start.2 = (bf16[1,1,32,2048]{3,2,1,0:T(8,128)(2,1)S(1)}, bf16[1,1,32,2048]{3,2,1,0:T(8,128)(2,1)S(1)}, u32[]{:S(2)}, u32[]{:S(2)}) collective-permute-start(bf16[1,1,32,2048]{3,2,1,0:T(8,128)(2,1)S(1)} %get-tuple-element.19), channel_id=1, source_target_pairs={{0,3},{1,2},{2,1},{3,0},{4,7},{5,6},{6,5},{7,4},{8,11},{9,10},{10,... | collective-permute-start | bytes 393224 | tf_op jit(solution)/shard_map/ppermute | solution.py:33
  18.8 7.0 %collective-permute-start.3 = (bf16[1,1,32,2048]{3,2,1,0:T(8,128)(2,1)S(1)}, bf16[1,1,32,2048]{3,2,1,0:T(8,128)(2,1)S(1)}, u32[]{:S(2)}, u32[]{:S(2)}) collective-permute-start(bf16[1,1,32,2048]{3,2,1,0:T(8,128)(2,1)S(1)} %get-tuple-element.18), channel_id=1, source_target_pairs={{0,4},{1,5},{2,6},{3,7},{4,0},{5,1},{6,2},{7,3},{8,12},{9,13},{10,... | collective-permute-start | bytes 393224 | tf_op jit(solution)/shard_map/ppermute | solution.py:33
  20.4 9.7 %collective-permute-start.4 = (bf16[1,1,32,2048]{3,2,1,0:T(8,128)(2,1)S(1)}, bf16[1,1,32,2048]{3,2,1,0:T(8,128)(2,1)S(1)}, u32[]{:S(2)}, u32[]{:S(2)}) collective-permute-start(bf16[1,1,32,2048]{3,2,1,0:T(8,128)(2,1)S(1)} %get-tuple-element.17), channel_id=1, source_target_pairs={{0,5},{1,4},{2,7},{3,6},{4,1},{5,0},{6,3},{7,2},{8,13},{9,12},{10,... | collective-permute-start | bytes 393224 | tf_op jit(solution)/shard_map/ppermute | solution.py:33
  20.8 12.9 %collective-permute-start.5 = (bf16[1,1,32,2048]{3,2,1,0:T(8,128)(2,1)S(1)}, bf16[1,1,32,2048]{3,2,1,0:T(8,128)(2,1)S(1)}, u32[]{:S(2)}, u32[]{:S(2)}) collective-permute-start(bf16[1,1,32,2048]{3,2,1,0:T(8,128)(2,1)S(1)} %get-tuple-element.16), channel_id=1, source_target_pairs={{0,6},{1,7},{2,4},{3,5},{4,2},{5,3},{6,0},{7,1},{8,14},{9,15},{10,... | collective-permute-start | bytes 393224 | tf_op jit(solution)/shard_map/ppermute | solution.py:33
  23.6 14.1 %collective-permute-start.6 = (bf16[1,1,32,2048]{3,2,1,0:T(8,128)(2,1)S(1)}, bf16[1,1,32,2048]{3,2,1,0:T(8,128)(2,1)S(1)}, u32[]{:S(2)}, u32[]{:S(2)}) collective-permute-start(bf16[1,1,32,2048]{3,2,1,0:T(8,128)(2,1)S(1)} %get-tuple-element.15), channel_id=1, source_target_pairs={{0,7},{1,6},{2,5},{3,4},{4,3},{5,2},{6,1},{7,0},{8,15},{9,14},{10,... | collective-permute-start | bytes 393224 | tf_op jit(solution)/shard_map/ppermute | solution.py:33
  24.8 14.1 %collective-permute-start.7 = (bf16[1,1,32,2048]{3,2,1,0:T(8,128)(2,1)S(1)}, bf16[1,1,32,2048]{3,2,1,0:T(8,128)(2,1)S(1)}, u32[]{:S(2)}, u32[]{:S(2)}) collective-permute-start(bf16[1,1,32,2048]{3,2,1,0:T(8,128)(2,1)S(1)} %get-tuple-element.14), channel_id=1, source_target_pairs={{0,8},{1,9},{2,10},{3,11},{4,12},{5,13},{6,14},{7,15},{8,0},{9,1},... | collective-permute-start | bytes 393224 | tf_op jit(solution)/shard_map/ppermute | solution.py:33
  25.8 23.7 %collective-permute-start.8 = (bf16[1,1,32,2048]{3,2,1,0:T(8,128)(2,1)S(1)}, bf16[1,1,32,2048]{3,2,1,0:T(8,128)(2,1)S(1)}, u32[]{:S(2)}, u32[]{:S(2)}) collective-permute-start(bf16[1,1,32,2048]{3,2,1,0:T(8,128)(2,1)S(1)} %get-tuple-element.13), channel_id=1, source_target_pairs={{0,9},{1,8},{2,11},{3,10},{4,13},{5,12},{6,15},{7,14},{8,1},{9,0},... | collective-permute-start | bytes 393224 | tf_op jit(solution)/shard_map/ppermute | solution.py:33
  30.1 22.6 %collective-permute-start.9 = (bf16[1,1,32,2048]{3,2,1,0:T(8,128)(2,1)S(1)}, bf16[1,1,32,2048]{3,2,1,0:T(8,128)(2,1)S(1)}, u32[]{:S(2)}, u32[]{:S(2)}) collective-permute-start(bf16[1,1,32,2048]{3,2,1,0:T(8,128)(2,1)S(1)} %get-tuple-element.12), channel_id=1, source_target_pairs={{0,10},{1,11},{2,8},{3,9},{4,14},{5,15},{6,12},{7,13},{8,2},{9,3},... | collective-permute-start | bytes 393224 | tf_op jit(solution)/shard_map/ppermute | solution.py:33
  33.7 24.4 %collective-permute-start.10 = (bf16[1,1,32,2048]{3,2,1,0:T(8,128)(2,1)S(1)}, bf16[1,1,32,2048]{3,2,1,0:T(8,128)(2,1)S(1)}, u32[]{:S(2)}, u32[]{:S(2)}) collective-permute-start(bf16[1,1,32,2048]{3,2,1,0:T(8,128)(2,1)S(1)} %get-tuple-element.11), channel_id=1, source_target_pairs={{0,11},{1,10},{2,9},{3,8},{4,15},{5,14},{6,13},{7,12},{8,3},{9,2},... | collective-permute-start | bytes 393224 | tf_op jit(solution)/shard_map/ppermute | solution.py:33
  37.7 28.2 %collective-permute-start.11 = (bf16[1,1,32,2048]{3,2,1,0:T(8,128)(2,1)S(1)}, bf16[1,1,32,2048]{3,2,1,0:T(8,128)(2,1)S(1)}, u32[]{:S(2)}, u32[]{:S(2)}) collective-permute-start(bf16[1,1,32,2048]{3,2,1,0:T(8,128)(2,1)S(1)} %get-tuple-element.10), channel_id=1, source_target_pairs={{0,12},{1,13},{2,14},{3,15},{4,8},{5,9},{6,10},{7,11},{8,4},{9,5},... | collective-permute-start | bytes 393224 | tf_op jit(solution)/shard_map/ppermute | solution.py:33
  38.9 29.8 %collective-permute-start.12 = (bf16[1,1,32,2048]{3,2,1,0:T(8,128)(2,1)S(1)}, bf16[1,1,32,2048]{3,2,1,0:T(8,128)(2,1)S(1)}, u32[]{:S(2)}, u32[]{:S(2)}) collective-permute-start(bf16[1,1,32,2048]{3,2,1,0:T(8,128)(2,1)S(1)} %get-tuple-element.9), channel_id=1, source_target_pairs={{0,13},{1,12},{2,15},{3,14},{4,9},{5,8},{6,11},{7,10},{8,5},{9,4},... | collective-permute-start | bytes 393224 | tf_op jit(solution)/shard_map/ppermute | solution.py:33
  49.6 22.5 %collective-permute-start.13 = (bf16[1,1,32,2048]{3,2,1,0:T(8,128)(2,1)S(1)}, bf16[1,1,32,2048]{3,2,1,0:T(8,128)(2,1)S(1)}, u32[]{:S(2)}, u32[]{:S(2)}) collective-permute-start(bf16[1,1,32,2048]{3,2,1,0:T(8,128)(2,1)S(1)} %get-tuple-element.8), channel_id=1, source_target_pairs={{0,14},{1,15},{2,12},{3,13},{4,10},{5,11},{6,8},{7,9},{8,6},{9,7},... | collective-permute-start | bytes 393224 | tf_op jit(solution)/shard_map/ppermute | solution.py:33
  52.6 22.2 %collective-permute-start.14 = (bf16[1,1,32,2048]{3,2,1,0:T(8,128)(2,1)S(1)}, bf16[1,1,32,2048]{3,2,1,0:T(8,128)(2,1)S(1)}, u32[]{:S(2)}, u32[]{:S(2)}) collective-permute-start(bf16[1,1,32,2048]{3,2,1,0:T(8,128)(2,1)S(1)} %get-tuple-element.7), channel_id=1, source_target_pairs={{0,15},{1,14},{2,13},{3,12},{4,11},{5,10},{6,9},{7,8},{8,7},{9,6},... | collective-permute-start | bytes 393224 | tf_op jit(solution)/shard_map/ppermute | solution.py:33
  79.1 4.5 %copy-start.1 = (bf16[16,32,2048]{2,1,0:T(8,128)(2,1)S(1)}, bf16[16,32,2048]{2,1,0:T(8,128)(2,1)}, u32[]{:S(2)}) copy-start(bf16[16,32,2048]{2,1,0:T(8,128)(2,1)} %gather_fusion.1) | copy-start | bytes 6291460
  79.1 4.5 %copy-start.3 = (bf16[1,2048,768]{2,1,0:T(8,128)(2,1)S(1)}, bf16[1,2048,768]{2,1,0:T(8,128)(2,1)}, u32[]{:S(2)}) copy-start(bf16[1,2048,768]{2,1,0:T(8,128)(2,1)} %param.10) | copy-start | bytes 9437188
  88.6 4.7 %copy-start.2 = (f32[128,8]{0,1:T(8,128)S(1)}, f32[128,8]{0,1:T(8,128)}, u32[]{:S(2)}) copy-start(f32[128,8]{0,1:T(8,128)} %param.8) | copy-start | bytes 12292
  88.6 52.4 %all-to-all-start = ((bf16[1,16,32,2048]{3,2,0,1:T(8,128)(2,1)}), bf16[1,16,32,2048]{3,2,0,1:T(8,128)(2,1)}, u32[]{:S(2)}, u32[]{:S(2)}) async-start(bf16[1,16,32,2048]{3,2,0,1:T(8,128)(2,1)} %convolution_bitcast_fusion), calls=%async_computation | async-start | bytes 4194304 | tf_op jit(solution)/shard_map/all_to_all | solution.py:69
